TPU v7x, 32 devices: a whole 2x2x4 slice. The times are simulated.
32 devices in a mesh: dp: 4 (over z), feat: 8 (over y, x, core).
Axes of the slice: x: 2, y: 2, z: 4, core: 2. Of those that a mesh axis runs over, the one named last changes fastest.
Arguments:
- clip_feats: bfloat16 [2, 384, 8192], P(None, 'dp', 'feat'), may hold values from 0 to 60
- proj_weight: bfloat16 [8192, 8192], P('dp', 'feat'), may hold values from -0.0625 to 0.0625
Outputs:
- loss_value: float32 [], replicated
- weight_grad: float32 [8192, 8192], P('dp', 'feat')
- redundancy: float32 [], replicated
- pair_similarity: float32 [384, 384], P('dp')
All inputs are finite; a program needn't handle non-finite values.
Results may differ from a plain program's by a relative error of at most 0.034.
Values may be sent and summed in bfloat16 or wider, within the bound.
A program may use at most 64 MiB of HBM per device.

v0:
```python
import math
import jax
import jax.numpy as jnp
from jax import lax
from jax.sharding import PartitionSpec as P

D = 8192
off_weight = 0.0051
epsilon = 1e-05
grad_scale = 32.0


def per_device(clip_feats, proj_weight):
    pairs = clip_feats.shape[1]
    width = clip_feats.shape[2]
    dp_count = lax.axis_size("dp")
    pair_count = float(pairs * dp_count)
    gathered = lax.all_gather(clip_feats, "feat", axis=2, tiled=True)
    stacked = gathered.reshape(2 * pairs, gathered.shape[2])
    projected = jnp.dot(
        stacked,
        lax.all_gather(proj_weight, "dp", axis=0, tiled=True),
        preferred_element_type=jnp.float32,
    ).reshape(2, pairs, width)
    col_mean = lax.psum(jnp.sum(projected, axis=1), "dp")[:, None, :] / pair_count
    centered = projected - col_mean
    col_var = lax.psum(jnp.sum(centered * centered, axis=1), "dp")[:, None, :] / pair_count
    col_scale = lax.rsqrt(col_var + epsilon)
    normed = centered * col_scale
    quantized = normed.astype(jnp.bfloat16)
    widened = quantized.astype(jnp.float32)
    batch_all = lax.all_gather(quantized, "dp", axis=1, tiled=True)
    gram_part = jnp.einsum("vpc,vnc->vpn", quantized, batch_all, preferred_element_type=jnp.float32)
    grams = lax.psum(gram_part, "feat")
    total_pairs = grams.shape[2]
    row_ids = (
        lax.broadcasted_iota(jnp.int32, (pairs, total_pairs), 0) + lax.axis_index("dp") * pairs
    )
    col_ids = lax.broadcasted_iota(jnp.int32, (pairs, total_pairs), 1)
    pair_similarity = jnp.where(
        row_ids == col_ids, 0.0, (grams[0] + grams[1]) / (2.0 * math.sqrt(float(D)))
    )
    diag_corr = lax.psum(jnp.sum(widened[0] * widened[1], axis=0), "dp") / pair_count
    frobenius = jnp.sum(grams[0] * grams[1])
    diag_term = jnp.sum((1.0 - diag_corr) ** 2 - off_weight * diag_corr * diag_corr)
    dp_first = (lax.axis_index("dp") == 0).astype(jnp.float32)
    feat_first = (lax.axis_index("feat") == 0).astype(jnp.float32)
    frob_scaled = feat_first * frobenius / (pair_count * pair_count)
    loss_term = dp_first * diag_term + off_weight * frob_scaled
    off_term = frob_scaled - dp_first * jnp.sum(diag_corr * diag_corr)
    total_loss, off_sum = lax.psum((loss_term, off_term), ("dp", "feat"))
    loss_value = 16.0 * total_loss / float(D)
    redundancy = 8.0 * pair_count * off_sum / (float(D) * float(D))
    slope = -2.0 * (1.0 - diag_corr) - 2.0 * off_weight * diag_corr
    coefficient = 2.0 * off_weight / (pair_count * pair_count)
    gram_q = grams.astype(jnp.bfloat16)
    cross_first = jnp.dot(gram_q[1], batch_all[0], preferred_element_type=jnp.float32)
    cross_second = jnp.dot(gram_q[0], batch_all[1], preferred_element_type=jnp.float32)
    grad_norm = jnp.stack(
        [
            slope * widened[1] / pair_count + coefficient * cross_first,
            slope * widened[0] / pair_count + coefficient * cross_second,
        ]
    )
    sum_one, sum_two = lax.psum(
        (jnp.sum(grad_norm, axis=1), jnp.sum(grad_norm * normed, axis=1)), "dp"
    )
    pre_grad = col_scale * (
        grad_norm - sum_one[:, None, :] / pair_count - normed * (sum_two[:, None, :] / pair_count)
    )
    pre_q = pre_grad.astype(jnp.bfloat16)
    flat_grad = pre_q.reshape(2 * pairs, width)
    summed = lax.psum_scatter(
        jnp.dot(stacked.T, flat_grad, preferred_element_type=jnp.float32).astype(jnp.bfloat16),
        "dp",
        scatter_dimension=0,
        tiled=True,
    ).astype(jnp.float32)
    return (loss_value, grad_scale * summed, redundancy, pair_similarity)


def solution(mesh):
    placed = (P(None, "dp", "feat"), P("dp", "feat"))
    return jax.shard_map(
        per_device,
        mesh=mesh,
        in_specs=placed,
        out_specs=(P(), P("dp", "feat"), P(), P("dp", None)),
        check_vma=False,
    )
```

profile of v0, /device:TPU:0, one launch (start us, length us, event | category | flops | bytes accessed | tf_op | source)
XLA Modules:
  0.0 791.4 jit_solution(3627898898711487195)
XLA Ops:
  7.2 0.7 all-gather.4.cloned.1.call-update
  7.9 0.7 all-gather.6.cloned.1.call-update
  8.7 36.3 %all-gather.4.cloned.1.call-done = bf16[2,96,8192]{2,1,0:T(8,128)(2,1)} async-done(((bf16[2,96,1024]{2,1,0:T(8,128)(2,1)}), bf16[2,96,8192]{2,1,0:T(8,128)(2,1)}) %all-gather.4.cloned.1.call-update) | async-done | bytes 3145744 | tf_op jit(solution)/shard_map/all_gather | solution.py:18
  45.0 288.4 %all-gather.6.cloned.1.call-done = bf16[8192,1024]{1,0:T(8,128)(2,1)} async-done(((bf16[2048,1024]{1,0:T(8,128)(2,1)}), bf16[8192,1024]{1,0:T(8,128)(2,1)}) %all-gather.6.cloned.1.call-update) | async-done | bytes 16777232 | tf_op jit(solution)/shard_map/all_gather | solution.py:22
  333.3 8.5 %fusion.16 = (f32[2,1024]{1,0:T(2,128)S(1)}, f32[2,96,1024]{2,1,0:T(8,128)S(1)}) fusion(bf16[2,96,8192]{2,1,0:T(8,128)(2,1)} %all-gather.4.cloned.1.call-done, bf16[8192,1024]{1,0:T(8,128)(2,1)} %all-gather.6.cloned.1.call-done), kind=kOutput, calls=%fused_computation.42 | convolution fusion | flops 3221420032 | bytes 20717568 | tf_op jit(solution)/shard_map/dot_general | solution.py:20
  341.8 8.8 %psum.56 = f32[2,1024]{1,0:T(2,128)S(1)} all-reduce(f32[2,1024]{1,0:T(2,128)S(1)} %get-tuple-element.19), channel_id=1, replica_groups=mesh['dp'=4,'feat'=8] {'dp'}, use_global_device_ids=true, to_apply=%region_1.0 | all-reduce | flops 2048 | bytes 16384 | tf_op jit(solution)/shard_map/psum | solution.py:25
  350.7 10.3 %psum.57 = f32[2,1024]{1,0:T(2,128)S(1)} all-reduce(f32[2,1024]{1,0:T(2,128)S(1)} %multiply_reduce_fusion.1), channel_id=1, replica_groups=mesh['dp'=4,'feat'=8] {'dp'}, use_global_device_ids=true, to_apply=%region_3.0 | all-reduce | flops 2048 | bytes 16384 | tf_op jit(solution)/shard_map/psum | solution.py:27
  361.1 0.9 fusion.14
  362.1 8.7 %psum.58 = f32[1024]{0:T(1024)S(1)} all-reduce(f32[1024]{0:T(1024)S(1)} %multiply_reduce_fusion.2), channel_id=1, replica_groups=mesh['dp'=4,'feat'=8] {'dp'}, use_global_device_ids=true, to_apply=%region_5.6 | all-reduce | flops 1024 | bytes 8192 | tf_op jit(solution)/shard_map/psum | solution.py:43
  370.8 26.6 %all-gather.8.cloned.1.call-done = bf16[2,384,1024]{2,1,0:T(8,128)(2,1)} async-done(((bf16[2,96,1024]{2,1,0:T(8,128)(2,1)}), bf16[2,384,1024]{2,1,0:T(8,128)(2,1)}) %all-gather.8.cloned.1.call-update) | async-done | bytes 1572880 | tf_op jit(solution)/shard_map/all_gather | solution.py:32
  397.3 3.0 fusion.17
  400.4 1.2 multiply_reduce_fusion.4
  401.6 50.8 %all-reduce.4.cloned.1.call-done = f32[2,96,384]{2,1,0:T(8,128)} async-done(((f32[2,96,384]{2,1,0:T(8,128)}), f32[2,96,384]{2,1,0:T(8,128)}) %all-reduce.4.cloned.1.call-update) | async-done | bytes 294928 | tf_op jit(solution)/shard_map/psum | solution.py:34
  452.4 1.0 convert_element_type.25
  453.4 1.4 fusion.4
  454.8 1.0 fusion.6
  455.8 0.7 copy-done.1
  456.8 18.7 %all-reduce.1 = (f32[2,1024]{1,0:T(2,128)S(1)}, f32[2,1024]{1,0:T(2,128)S(1)}) all-reduce(f32[2,1024]{1,0:T(2,128)S(1)} %get-tuple-element.9, f32[2,1024]{1,0:T(2,128)S(1)} %get-tuple-element.8), channel_id=1, replica_groups=mesh['dp'=4,'feat'=8] {'dp'}, use_global_device_ids=true, to_apply=%region_13.14 | all-reduce | flops 4096 | bytes 32768 | tf_op jit(solution)/shard_map/psum | solution.py:65
  475.5 12.4 %fusion.2 = bf16[8192,1024]{0,1:T(8,128)(2,1)} fusion(bf16[2,96,8192]{2,1,0:T(8,128)(2,1)} %all-gather.4.cloned.1.call-done, f32[2,96,1024]{2,1,0:T(8,128)S(1)} %get-tuple-element.20, f32[1,96,1024]{2,1,0:T(8,128)S(1)} %fusion.4, f32[1,96,1024]{2,1,0:T(8,128)} %copy-done.1, f32[2,1024]{1,0:T(2,128)S(1)} %get-tuple-element.21, ...), kind=kOutput, calls=%fused_computation.3 | convolution fusion | flops 3231186944 | bytes 21528576 | tf_op jit(solution)/shard_map/dot_general | solution.py:74
  490.6 41.4 %all-reduce = (f32[]{:T(128)}, f32[]{:T(128)}) all-reduce(f32[]{:T(128)S(6)} %add.47, f32[]{:T(128)S(6)} %sub.40), channel_id=1, replica_groups=mesh['dp'=4,'feat'=8] {'dp','feat'}, use_global_device_ids=true, to_apply=%region_9.10 | all-reduce | flops 2 | bytes 16 | tf_op jit(solution)/shard_map/psum | solution.py:51
  533.3 0.7 bitcast_select_fusion
  534.0 232.7 %reduce-scatter.2.cloned.1.call-done = bf16[2048,1024]{0,1:T(8,128)(2,1)} async-done(((bf16[8192,1024]{0,1:T(8,128)(2,1)}), bf16[2048,1024]{0,1:T(8,128)(2,1)}) %reduce-scatter.2.cloned.1.call-update) | async-done | bytes 4194320 | tf_op jit(solution)/shard_map/reduce_scatter | solution.py:73
  766.7 6.6 convert_multiply_fusion
  773.4 9.2 %copy.6 = f32[2048,1024]{1,0:T(8,128)} copy(f32[2048,1024]{0,1:T(8,128)} %convert_multiply_fusion) | data formatting | bytes 16777216
  (21 shorter events, 1.3 us)
Async XLA Ops:
  7.2 37.8 %all-gather.4.cloned.1.call-start = ((), (), s32[]{:S(2)}) async-start(), calls=%async_computation.1 | async-start | bytes 3538944 | tf_op jit(solution)/shard_map/all_gather | solution.py:18
  7.9 325.4 %all-gather.6.cloned.1.call-start = ((), (), s32[]{:S(2)}) async-start(), calls=%async_computation.2 | async-start | bytes 20971520 | tf_op jit(solution)/shard_map/all_gather | solution.py:22
  8.6 388.7 %all-gather.8.cloned.1.call-start = ((), (), s32[]{:S(2)}) async-start(), calls=%async_computation.3 | async-start | bytes 1966080 | tf_op jit(solution)/shard_map/all_gather | solution.py:32
  362.0 90.4 %all-reduce.4.cloned.1.call-start = ((), (), s32[]{:S(2)}) async-start(), calls=%async_computation.4 | async-start | bytes 589824 | tf_op jit(solution)/shard_map/psum | solution.py:34
  397.3 57.5 %copy-start = (bf16[2,384,1024]{2,1,0:T(8,128)(2,1)S(1)}, bf16[2,384,1024]{2,1,0:T(8,128)(2,1)}, u32[]{:S(2)}) copy-start(bf16[2,384,1024]{2,1,0:T(8,128)(2,1)} %all-gather.8.cloned.1.call-done) | copy-start | bytes 4718596
  400.3 366.4 %reduce-scatter.2.cloned.1.call-start = ((), (), s32[]{:S(2)}) async-start(), calls=%async_computation.5 | async-start | bytes 20971520 | tf_op jit(solution)/shard_map/reduce_scatter | solution.py:73
  455.8 0.7 copy-start.1
  487.9 1.4 copy-start.2
Sparse Core Ops, SparseCore 0:
  9.9 35.0 all-gather.3
  46.5 286.7 all-gather.5
  362.1 35.1 all-gather.7
  400.5 51.9 all-reduce.3
  488.0 278.6 reduce-scatter.1
where the time goes:
time: 792 us; the launch traced here: 791 us
  waiting for transfers between devices  636 us (80%)
  blocking collectives  87.9 us (11%)
  matrix products  26.2 us (3%)
  between operations  19.5 us (2%)
  other arithmetic  11.4 us (1%)
  local copies, waits for them, and re-layouts  9.99 us (1%)
    all_gather x1, waiting for transfers between devices, per_device(): lax.all_gather(proj_weight, 'dp', axis=0, tiled=True)  288 us
    reduce_scatter x1, waiting for transfers between devices, per_device(): lax.psum_scatter(jnp.dot(stacked.T, flat_grad, preferred_element_type=jnp...  233 us
    psum x1, waiting for transfers between devices, per_device(): grams = lax.psum(gram_part, 'feat')  50.8 us
    psum x1, blocking collectives, per_device(): total_loss, off_sum = lax.psum((loss_term, off_term), ('dp', 'feat'))  41.4 us
    all_gather x1, waiting for transfers between devices, per_device(): gathered = lax.all_gather(clip_feats, 'feat', axis=2, tiled=True)  36.3 us
    all_gather x1, waiting for transfers between devices, per_device(): batch_all = lax.all_gather(quantized, 'dp', axis=1, tiled=True)  26.6 us
    psum x1, blocking collectives, per_device(): lax.psum((jnp.sum(grad_norm, axis=1), jnp.sum(grad_norm * normed, axis=1)...  18.7 us
  transfers between devices with their start and end apart: 5, of which 5 were waited for; matrix products, arithmetic and copies ran while one was open for 0% of the time, Pallas kernels for 0%

commit v1 on v0

--- a/solution.py
+++ b/solution.py
@@ -11,6 +11,20 @@
 
 
 def per_device(clip_feats, proj_weight):
+
+    def obtain_seats_all(body):
+        arr_out = lax.axis_size("dp")
+        mat_out = lax.axis_index("dp")
+        g_now, main, val2 = (arr_out, mat_out, body.shape[0])
+        mixed_arr, u_next = (body, 1)
+        while u_next < g_now:
+            long_array = range(g_now)
+            x_new = map(lambda dev_j: (dev_j, (dev_j - u_next) % g_now), long_array)
+            parts_out = lax.ppermute(mixed_arr, "dp", list(x_new))
+            mixed_arr = jnp.concatenate([mixed_arr, parts_out], axis=0)
+            u_next = 2 * u_next
+        return jnp.roll(mixed_arr, main * val2, axis=0)
+
     pairs = clip_feats.shape[1]
     width = clip_feats.shape[2]
     dp_count = lax.axis_size("dp")
@@ -18,9 +32,7 @@
     gathered = lax.all_gather(clip_feats, "feat", axis=2, tiled=True)
     stacked = gathered.reshape(2 * pairs, gathered.shape[2])
     projected = jnp.dot(
-        stacked,
-        lax.all_gather(proj_weight, "dp", axis=0, tiled=True),
-        preferred_element_type=jnp.float32,
+        stacked, obtain_seats_all(proj_weight), preferred_element_type=jnp.float32
     ).reshape(2, pairs, width)
     col_mean = lax.psum(jnp.sum(projected, axis=1), "dp")[:, None, :] / pair_count
     centered = projected - col_mean

time: 792 us -> 953 us (1.20)
  waiting for transfers between devices: 636 us -> 752 us
  local copies, waits for them, and re-layouts: 9.99 us -> 40.5 us
    ppermute x0 -> x2, waiting for transfers between devices: none -> 442 us  [obtain_seats_all(): parts_out = lax.ppermute(mixed_arr, 'dp', list(x_new))]
    all_gather x1 -> x0, waiting for transfers between devices: 288 us -> none  [per_device(): lax.all_gather(proj_weight, 'dp', axis=0, tiled=True)]
    all_gather x1, waiting for transfers between devices: 36.3 us -> 0.01 us  [per_device(): gathered = lax.all_gather(clip_feats, 'feat', axis=2, tiled=True)]
    unnamed x7 -> x10, local copies, waits for them, and re-layouts: 9.99 us -> 32.9 us
  transfers between devices with their start and end apart: 5 -> 6, of which waited for: 5 -> 5; matrix products, arithmetic and copies ran while one was open for 0% -> 3% of each run, Pallas kernels for 0% -> 0%
where the time goes in v1:
time: 953 us; the launch traced here: 952 us
  waiting for transfers between devices  752 us (79%)
  blocking collectives  90.1 us (9%)
  local copies, waits for them, and re-layouts  40.5 us (4%)
  matrix products  24.2 us (3%)
  between operations  19.5 us (2%)
  other arithmetic  18.8 us (2%)
    ppermute x2, waiting for transfers between devices, obtain_seats_all(): parts_out = lax.ppermute(mixed_arr, 'dp', list(x_new))  442 us
    reduce_scatter x1, waiting for transfers between devices, per_device(): lax.psum_scatter(jnp.dot(stacked.T, flat_grad, preferred_element_type=jnp...  233 us
    psum x1, waiting for transfers between devices, per_device(): grams = lax.psum(gram_part, 'feat')  51.5 us
    psum x1, blocking collectives, per_device(): total_loss, off_sum = lax.psum((loss_term, off_term), ('dp', 'feat'))  41.4 us
    unnamed x10, local copies, waits for them, and re-layouts  32.9 us
    all_gather x1, waiting for transfers between devices, per_device(): batch_all = lax.all_gather(quantized, 'dp', axis=1, tiled=True)  26.3 us
  transfers between devices with their start and end apart: 6, of which 5 were waited for; matrix products, arithmetic and copies ran while one was open for 3% of the time, Pallas kernels for 0%

profile of v1, /device:TPU:0, one launch (start us, length us, event | category | flops | bytes accessed | tf_op | source)
XLA Modules:
  0.0 952.1 jit_solution(18072599116478136054)
XLA Ops:
  7.2 5.1 collective-permute-start
  12.3 90.1 %collective-permute-done = bf16[2048,1024]{1,0:T(8,128)(2,1)} collective-permute-done((bf16[2048,1024]{1,0:T(8,128)(2,1)}, bf16[2048,1024]{1,0:T(8,128)(2,1)}, u32[]{:S(2)}, u32[]{:S(2)}) %collective-permute-start) | collective-permute-done | bytes 4194336 | tf_op jit(solution)/shard_map/ppermute | solution.py:23
  102.5 7.8 pad_maximum_fusion
  110.3 1.5 collective-permute-start.1
  111.9 4.6 constant_dynamic-update-slice_fusion.5
  116.4 4.6 constant_dynamic-update-slice_fusion.4
  121.0 351.6 %collective-permute-done.1 = bf16[4096,1024]{1,0:T(8,128)(2,1)} collective-permute-done((bf16[4096,1024]{1,0:T(8,128)(2,1)}, bf16[4096,1024]{1,0:T(8,128)(2,1)}, u32[]{:S(2)}, u32[]{:S(2)}) %collective-permute-start.1) | collective-permute-done | bytes 8388640 | tf_op jit(solution)/shard_map/ppermute | solution.py:23
  472.6 7.6 constant_dynamic-update-slice_fusion.3
  480.2 2.4 constant_dynamic-update-slice_fusion.2
  482.5 4.6 constant_dynamic-update-slice_fusion.1
  487.1 7.6 constant_dynamic-update-slice_fusion
  494.7 8.5 fusion
  503.3 11.0 %psum.56 = f32[2,1024]{1,0:T(2,128)S(1)} all-reduce(f32[2,1024]{1,0:T(2,128)S(1)} %reduce_sum.72), channel_id=1, replica_groups=mesh['dp'=4,'feat'=8] {'dp'}, use_global_device_ids=true, to_apply=%region_1.2 | all-reduce | flops 2048 | bytes 16384 | tf_op jit(solution)/shard_map/psum | solution.py:37
  514.3 8.5 psum.57
  523.9 10.5 %psum.58 = f32[1024]{0:T(1024)S(1)} all-reduce(f32[1024]{0:T(1024)S(1)} %multiply_reduce_fusion.2), channel_id=1, replica_groups=mesh['dp'=4,'feat'=8] {'dp'}, use_global_device_ids=true, to_apply=%region_5.6 | all-reduce | flops 1024 | bytes 8192 | tf_op jit(solution)/shard_map/psum | solution.py:55
  534.4 26.3 %all-gather.5.cloned.1.call-done = bf16[2,384,1024]{2,1,0:T(8,128)(2,1)} async-done(((bf16[2,96,1024]{2,1,0:T(8,128)(2,1)}), bf16[2,384,1024]{2,1,0:T(8,128)(2,1)}) %all-gather.5.cloned.1.call-update) | async-done | bytes 1572880 | tf_op jit(solution)/shard_map/all_gather | solution.py:44
  560.7 2.8 fusion.17
  564.2 51.5 %all-reduce.4.cloned.1.call-done = f32[2,96,384]{2,1,0:T(8,128)} async-done(((f32[2,96,384]{2,1,0:T(8,128)}), f32[2,96,384]{2,1,0:T(8,128)}) %all-reduce.4.cloned.1.call-update) | async-done | bytes 294928 | tf_op jit(solution)/shard_map/psum | solution.py:46
  619.8 18.7 %all-reduce.1 = (f32[2,1024]{1,0:T(2,128)S(1)}, f32[2,1024]{1,0:T(2,128)S(1)}) all-reduce(f32[2,1024]{1,0:T(2,128)S(1)} %get-tuple-element.9, f32[2,1024]{1,0:T(2,128)S(1)} %get-tuple-element.8), channel_id=1, replica_groups=mesh['dp'=4,'feat'=8] {'dp'}, use_global_device_ids=true, to_apply=%region_13.14 | all-reduce | flops 4096 | bytes 32768 | tf_op jit(solution)/shard_map/psum | solution.py:77
  638.6 10.0 %fusion.2 = bf16[8192,1024]{0,1:T(8,128)(2,1)} fusion(bf16[2,96,8192]{2,1,0:T(8,128)(2,1)} %all-gather.3.cloned.1.call-done, f32[2,96,1024]{2,1,0:T(8,128)S(1)} %bitcast.48, f32[1,96,1024]{2,1,0:T(8,128)S(1)} %fusion.4, f32[1,96,1024]{2,1,0:T(8,128)S(1)} %fusion.6, f32[2,1024]{1,0:T(2,128)S(1)} %get-tuple-element.19, f32[2,1024]{1,0:T(2,128)S(1)} %get-tuple-element.20, ...), kind=kOutput, calls=%fused_computation.3 | convolution fusion | flops 3231186944 | bytes 21528576 | tf_op jit(solution)/shard_map/dot_general | solution.py:86
  651.3 41.4 %all-reduce = (f32[]{:T(128)}, f32[]{:T(128)}) all-reduce(f32[]{:T(128)S(6)} %add.59, f32[]{:T(128)S(6)} %sub.45), channel_id=1, replica_groups=mesh['dp'=4,'feat'=8] {'dp','feat'}, use_global_device_ids=true, to_apply=%region_9.10 | all-reduce | flops 2 | bytes 16 | tf_op jit(solution)/shard_map/psum | solution.py:63
  694.8 232.7 %reduce-scatter.2.cloned.1.call-done = bf16[2048,1024]{0,1:T(8,128)(2,1)} async-done(((bf16[8192,1024]{0,1:T(8,128)(2,1)}), bf16[2048,1024]{0,1:T(8,128)(2,1)}) %reduce-scatter.2.cloned.1.call-update) | async-done | bytes 4194320 | tf_op jit(solution)/shard_map/reduce_scatter | solution.py:85
  927.5 6.6 convert_multiply_fusion
  934.1 9.2 copy.6
  (28 shorter events, 7.4 us)
Async XLA Ops:
  7.2 487.5 %all-gather.3.cloned.1.call-start = ((), (), s32[]{:S(2)}) async-start(), calls=%async_computation.1 | async-start | bytes 3538944 | tf_op jit(solution)/shard_map/all_gather | solution.py:32
  7.2 95.2 %collective-permute-start = (bf16[2048,1024]{1,0:T(8,128)(2,1)}, bf16[2048,1024]{1,0:T(8,128)(2,1)}, u32[]{:S(2)}, u32[]{:S(2)}) collective-permute-start(bf16[2048,1024]{1,0:T(8,128)(2,1)} %param.3), channel_id=1, source_target_pairs={{0,24},{8,0},{16,8},{24,16},{1,25},{9,1},{17,9},{25,17},{2,26},{10... | collective-permute-start | bytes 12582920 | tf_op jit(solution)/shard_map/ppermute | solution.py:23
  110.3 362.3 %collective-permute-start.1 = (bf16[4096,1024]{1,0:T(8,128)(2,1)}, bf16[4096,1024]{1,0:T(8,128)(2,1)}, u32[]{:S(2)}, u32[]{:S(2)}) collective-permute-start(bf16[4096,1024]{1,0:T(8,128)(2,1)} %pad_maximum_fusion), channel_id=1, source_target_pairs={{0,16},{8,24},{16,0},{24,8},{1,17},{9,25},{17,1},{25,9},{2,18},{10... | collective-permute-start | bytes 25165832 | tf_op jit(solution)/shard_map/ppermute | solution.py:23
  111.8 448.9 %all-gather.5.cloned.1.call-start = ((), (), s32[]{:S(2)}) async-start(), calls=%async_computation.2 | async-start | bytes 1966080 | tf_op jit(solution)/shard_map/all_gather | solution.py:44
  121.0 359.2 %copy-start = (bf16[2048,1024]{1,0:T(8,128)(2,1)S(1)}, bf16[2048,1024]{1,0:T(8,128)(2,1)}, u32[]{:S(2)}) copy-start(bf16[2048,1024]{1,0:T(8,128)(2,1)} %param.3) | copy-start | bytes 12582916
  523.8 92.0 %all-reduce.4.cloned.1.call-start = ((), (), s32[]{:S(2)}) async-start(), calls=%async_computation.3 | async-start | bytes 589824 | tf_op jit(solution)/shard_map/psum | solution.py:46
  563.6 363.9 %reduce-scatter.2.cloned.1.call-start = ((), (), s32[]{:S(2)}) async-start(), calls=%async_computation.4 | async-start | bytes 20971520 | tf_op jit(solution)/shard_map/reduce_scatter | solution.py:85
  648.6 1.4 copy-start.1
Sparse Core Ops, SparseCore 0:
  111.9 33.3 all-gather.2
  523.9 36.7 all-gather.4
  563.8 51.9 all-reduce.3
  648.8 278.6 reduce-scatter.1
